TPU v7x, 32 devices: a whole 2x2x4 slice. The times are simulated.
32 devices in a mesh: gx: 8 (over z, y), gy: 4 (over x, core).
Axes of the slice: x: 2, y: 2, z: 4, core: 2. Of those that a mesh axis runs over, the one named last changes fastest.
Arguments:
- coarse_send: bfloat16 [8, 35, 4096], P('gx', None, 'gy'), may hold values from -6 to 6
- coarse_flux: float32 [8, 35, 1024], P('gx', None, 'gy'), may hold values from -6 to 6
- patch_owner: int32 [8], replicated, may hold values from 0 to 15, as said below
- velocity: float32 [3], replicated, may hold values from -0.6 to 0.6
- diffusivity: float32 [35], replicated, may hold values from 0.03 to 0.15
- stoich: float32 [35, 35], replicated, may hold values from -1 to 1
Outputs:
- fine_state: float32 [16, 35, 32768], P('gx', None, 'gy')
- reflux: float32 [8, 35, 1024], P('gx', None, 'gy')
Inputs may be any that keep to these rules, and one draw needn't show every extreme that they name: `patch_owner`: the 8 entries are distinct; slot s belongs to owner group s // 2, the group of index s // 2 along gx; a group owns 0, 1 or 2 patches, and at least one group owns exactly 2.
All inputs are finite; a program needn't handle non-finite values.
Results may differ from a plain program's by a relative error of at most 0.0003.
Values may be sent and summed in bfloat16 or wider, within the bound.
No kernel may reach another device: no remote copies, remote signals or barrier semaphores. Data moves between devices by JAX's collectives and lax.ppermute only.
A program may use at most 128 MiB of HBM per device.

v0:
```python
import jax
import jax.numpy as jnp
from jax import lax
from jax.sharding import PartitionSpec as P

CB = 16
time_step = 0.25
heat_gain = 2.0
highest = lax.Precision.HIGHEST


def padded(block, sides, width):
    for axis, dim in sides:
        count = lax.axis_size(axis)
        forward = [(i, i + 1) for i in range(count - 1)]
        backward = [(target, source) for source, target in forward]
        low = lax.ppermute(
            lax.slice_in_dim(block, block.shape[dim] - width, None, axis=dim), axis, forward
        )
        high = lax.ppermute(lax.slice_in_dim(block, 0, width, axis=dim), axis, backward)
        block = jnp.concatenate([low, block, high], axis=dim)
    return block


def axis_slope(values, axis):
    moved = jnp.moveaxis(values, axis, 0)
    middle = (moved[2:] - moved[:-2]) * 0.5
    joined = jnp.concatenate([moved[1:2] - moved[0:1], middle, moved[-1:] - moved[-2:-1]], 0)
    return jnp.moveaxis(joined, 0, axis)


def spread(values):
    return values[..., :, None, :, None, :, None]


def refine(coarse, slope_z, slope_y, slope_x):
    offsets = jnp.array([-0.5, 0.5], jnp.float32)
    leading = coarse.shape[:-3]
    depth, height, breadth = coarse.shape[-3:]
    shift_y = offsets[:, None, None]
    shift_z = offsets[:, None, None, None, None]
    terms = spread(slope_x) * offsets + spread(slope_y) * shift_y + spread(slope_z) * shift_z
    fine_cells = spread(coarse) + terms * 0.5
    return fine_cells.reshape(leading + (2 * depth, 2 * height, 2 * breadth))


def face_flux(left_side, right_side, speed, diffuse):
    return speed * (left_side + right_side) * 0.5 - diffuse * (right_side - left_side)


def tendency(padded_layers, cells, velocity, diffusivity, stoich):
    diffuse = diffusivity[:, None, None, None]
    padded_cols = jnp.concatenate([cells[..., :1], cells, cells[..., -1:]], -1)
    padded_rows = jnp.concatenate([cells[..., :1, :], cells, cells[..., -1:, :]], -2)
    flux_cols = face_flux(padded_cols[..., :-1], padded_cols[..., 1:], velocity[0], diffuse)
    flux_rows = face_flux(padded_rows[..., :-1, :], padded_rows[..., 1:, :], velocity[1], diffuse)
    flux_layers = face_flux(
        padded_layers[..., :-1, :, :], padded_layers[..., 1:, :, :], velocity[2], diffuse
    )
    outflow = (
        flux_cols[..., 1:]
        - flux_cols[..., :-1]
        + (flux_rows[..., 1:, :] - flux_rows[..., :-1, :])
        + (flux_layers[..., 1:, :, :] - flux_layers[..., :-1, :, :])
    )
    reaction_rate = cells * jax.nn.sigmoid(heat_gain * cells[..., 0:1, :, :, :])
    source = jnp.einsum("fg,...gzyx->...fzyx", stoich, reaction_rate, precision=highest)
    side_fluxes = (
        flux_cols[..., 0],
        flux_cols[..., -1],
        flux_rows[..., 0, :],
        flux_rows[..., -1, :],
    )
    return (source - outflow, side_fluxes)


def tendency_slots(padded_layers, cells, velocity, diffusivity, stoich):

    def tendency_one_slot(pair):
        return tendency(pair[0], pair[1], velocity, diffusivity, stoich)

    return lax.map(tendency_one_slot, (padded_layers, cells))


def refine_slots(coarse, slope_z):

    def refine_one_slot(pair):
        block, slope_layers = pair
        return refine(block, slope_layers, axis_slope(block, 2), axis_slope(block, 3))

    return lax.map(refine_one_slot, (coarse, slope_z))


def average_sides(earlier, later_sides):
    return jnp.stack(
        [
            (earlier[0] + later_sides[0]) * 0.5,
            (earlier[1] + later_sides[1]) * 0.5,
            (earlier[2] + later_sides[2]) * 0.5,
            (earlier[3] + later_sides[3]) * 0.5,
        ],
        -2,
    )


def coarsen_faces(register):
    leading = register.shape[:-3]
    depth = register.shape[-3] // 2
    along = register.shape[-1] // 2
    split_faces = register.reshape(leading + (depth, 2, 4, along, 2))
    return (
        split_faces[..., 0, :, :, 0]
        + split_faces[..., 0, :, :, 1]
        + split_faces[..., 1, :, :, 0]
        + split_faces[..., 1, :, :, 1]
    ) * 0.25


def route_home(values, patch_owner, my_slots):
    chooser = (patch_owner[:, None] == my_slots[None, :]).astype(jnp.float32)
    return jnp.einsum("qo,ofc->qfc", chooser, values, precision=highest)


def shards(coarse_send, coarse_flux, patch_owner, velocity, diffusivity, stoich):
    send_slots, fields, layer_cells = coarse_send.shape
    own_slots = 2 * send_slots
    owner_group = lax.axis_index("gx")
    pencil = lax.axis_index("gy")
    pencils = lax.axis_size("gy")
    block_edge = CB
    layers = layer_cells // (block_edge * block_edge)
    my_slots = owner_group * own_slots + jnp.arange(own_slots, dtype=jnp.int32)
    chooser = (my_slots[:, None] == patch_owner[None, :]).astype(jnp.bfloat16)
    gathered = jnp.einsum(
        "oq,qfc->ofc",
        chooser,
        lax.all_gather(coarse_send, "gx", axis=0, tiled=True),
        preferred_element_type=jnp.float32,
    )
    coarse = gathered.reshape(own_slots, fields, layers, block_edge, block_edge)
    rimmed = padded(coarse.astype(jnp.bfloat16), (("gy", 2),), 1).astype(coarse.dtype)
    below = rimmed[:, :, :-2]
    above = rimmed[:, :, 2:]
    depth_index = pencil * layers + jnp.arange(layers, dtype=jnp.int32)
    is_first = (depth_index == 0)[:, None, None]
    is_last = (depth_index == block_edge - 1)[:, None, None]
    slope_z = jnp.where(
        is_first, above - coarse, jnp.where(is_last, coarse - below, (above - below) * 0.5)
    )
    fine_cells = refine_slots(coarse, slope_z)
    at_bottom = pencil == 0
    at_top = pencil == pencils - 1

    def extend_layers(cells):
        ghosts = padded(cells.astype(jnp.bfloat16), (("gy", 2),), 1).astype(cells.dtype)
        lower_ghost = jnp.where(at_bottom, cells[:, :, :1], ghosts[:, :, :1])
        upper_ghost = jnp.where(at_top, cells[:, :, -1:], ghosts[:, :, -1:])
        return jnp.concatenate([lower_ghost, cells, upper_ghost], 2)

    change, first_sides = tendency_slots(
        extend_layers(fine_cells), fine_cells, velocity, diffusivity, stoich
    )
    section_state = fine_cells + time_step * change
    second, second_sides = tendency_slots(
        extend_layers(section_state), section_state, velocity, diffusivity, stoich
    )
    final_state = fine_cells + time_step * 0.5 * (change + second)
    register = average_sides(first_sides, second_sides)
    flat_faces = coarsen_faces(register).reshape(own_slots, fields, -1)
    summed = lax.psum_scatter(
        route_home(flat_faces, patch_owner, my_slots), "gx", scatter_dimension=0, tiled=True
    )
    averaged = summed.reshape(send_slots, fields, layers, 4, block_edge)
    corrected = averaged - coarse_flux.reshape(send_slots, fields, layers, 4, block_edge)
    return (final_state.reshape(own_slots, fields, -1), corrected.reshape(send_slots, fields, -1))


def solution(mesh):
    placed = (P("gx", None, "gy"), P("gx", None, "gy"), P(), P(), P(), P())
    return jax.shard_map(
        shards,
        mesh=mesh,
        in_specs=placed,
        out_specs=(P("gx", None, "gy"), P("gx", None, "gy")),
        check_vma=False,
    )
```

profile of v0, /device:TPU:0, one launch (start us, length us, event | category | flops | bytes accessed | tf_op | source)
XLA Modules:
  0.0 392.6 jit_solution(8805554592416697023)
XLA Ops:
  7.2 33.6 %all_gather.3 = bf16[8,35,1024]{2,1,0:T(8,128)(2,1)S(1)} all-gather(bf16[1,35,1024]{2,1,0:T(8,128)(2,1)} %param.13), channel_id=1, replica_groups=mesh['gx'=8,'gy'=4] {'gx'}, dimensions={0}, use_global_device_ids=true | all-gather | bytes 645120 | tf_op jit(solution)/shard_map/all_gather | solution.py:137
  45.1 3.6 collective-permute-done.1
  49.3 4.5 %broadcast.182.clone = f32[2,35,8,32,32]{1,4,3,2,0:T(8,128)} broadcast(f32[]{:T(128)} %constant.54.clone.1), dimensions={} | broadcast | bytes 2293764 | tf_op jit(solution)/shard_map/broadcast.31
  53.8 17.1 %while.49 = (s32[]{:T(128)}, f32[2,35,8,32,32]{1,4,3,2,0:T(8,128)}, f32[2,35,4,16,16]{1,4,3,2,0:T(8,128)S(1)}, f32[2,35,4,16,16]{1,4,3,2,0:T(8,128)S(1)}, s32[]{:T(128)}, /*index=5*/f32[2]{0:T(128)S(1)}) while((s32[]{:T(128)}, f32[2,35,8,32,32]{1,4,3,2,0:T(8,128)}, f32[2,35,4,16,16]{1,4,3,2,0:T(8,128)S(1)}, ...), condition=%wide.region_1.2_spmd.clone, body=%wide.region_0.1_spmd.sunk.clone.sunk | while | flops 1496322 | bytes 12653153 | solution.py:91
  70.9 4.5 %convert_element_type.22 = bf16[2,35,8,32,32]{1,4,3,2,0:T(8,128)(2,1)S(1)} convert(f32[2,35,8,32,32]{1,4,3,2,0:T(8,128)} %get-tuple-element.589) | non-fusion elementwise | flops 573440 | bytes 3440640 | tf_op jit(solution)/shard_map/convert_element_type | solution.py:155
  77.5 5.5 %collective-permute-start.2 = (bf16[2,35,1,32,32]{1,4,3,2,0:T(8,128)(2,1)S(1)}, bf16[2,35,1,32,32]{1,4,3,2,0:T(8,128)(2,1)S(1)}, u32[]{:S(2)}, u32[]{:S(2)}) collective-permute-start(bf16[2,35,1,32,32]{1,4,3,2,0:T(8,128)(2,1)S(1)} %get-tuple-element.338), channel_id=1, source_target_pairs={{0,1},{1,2},{2,3},{4,5},{5,6},{6,7},{8,9},{9,10},{10,11},{12,13},{... | collective-permute-start | bytes 430088 | tf_op jit(solution)/shard_map/ppermute | solution.py:17
  88.7 9.3 %pad_maximum_fusion.8 = f32[2,35,10,32,32]{1,4,3,2,0:T(8,128)} fusion(f32[2,35,1,32,32]{1,4,3,2,0:T(8,128)S(1)} %get-tuple-element.335, f32[2,35,8,32,32]{1,4,3,2,0:T(8,128)} %get-tuple-element.589, f32[2,35,1,32,32]{1,4,3,2,0:T(8,128)S(1)} %get-tuple-element.334), kind=kLoop, calls=%fused_computation.78 | loop fusion | flops 1433600 | bytes 5734400 | tf_op jit(solution)/shard_map/concatenate | solution.py:158
  98.0 4.4 %broadcast.182.clone.1 = f32[2,35,8,32,32]{1,4,3,2,0:T(8,128)} broadcast(f32[]{:T(128)} %constant.54.clone.1), dimensions={} | broadcast | bytes 2293764 | tf_op jit(solution)/shard_map/broadcast.31
  102.5 81.6 %while.47 = (s32[]{:T(128)}, f32[2,35,8,32,32]{1,4,3,2,0:T(8,128)}, f32[2,35,8,32]{1,3,2,0:T(8,128)S(1)}, f32[2,35,8,32]{1,3,2,0:T(8,128)S(1)}, f32[2,35,8,32]{1...) while((s32[]{:T(128)}, f32[2,35,8,32,32]{1,4,3,2,0:T(8,128)}, ...), condition=%wide.region_3.4_spmd, body=%wide.region_2.3_spmd.sunk | while | flops 129128448 | bytes 80370104 | solution.py:82
  106.5 4.4 %multiply_subtract_fusion.14 = f32[35,8,32,33]{0,3,2,1:T(8,128)} fusion(f32[35,8,32,1]{0,3,2,1:T(1,128)S(1)} %get-tuple-element.523, f32[35,8,32,32]{0,3,2,1:T(8,128)S(1)} %dynamic-slice_bitcast_fusion.15, f32[35,8,32,1]{0,3,2,1:T(1,128)S(1)} %get-tuple-element.524, f32[35]{0:T(128)S(1)} %get-tuple-element.616, f32[]{:T(128)} %bitcast.137), kind=kLoop, calls=%fused_computation.3.clone.1 | loop fusion | flops 2365440 | bytes 2401424 | tf_op jit(solution)/shard_map/while/body/eval_jaxpr/sub | solution.py:48
  110.9 3.4 multiply_subtract_fusion.13
  115.0 3.7 multiply_subtract_fusion.12
  118.7 4.6 %constant_dynamic-slice_fusion.4 = f32[1,1,8,32,32]{1,4,3,2,0:T(8,128)} fusion(f32[2,35,8,32,32]{1,4,3,2,0:T(8,128)} %get-tuple-element.613, s32[]{:T(128)} %get-tuple-element.595), kind=kLoop, calls=%fused_computation.26.clone.1 | loop fusion | bytes 65540 | tf_op jit(solution)/shard_map/while/body/eval_jaxpr/slice | solution.py:66
  126.5 14.0 %fusion.78 = f32[2,35,8,32,32]{1,4,3,2,0:T(8,128)} fusion(f32[2,35,8,32,32]{1,4,3,2,0:T(8,128)} %get-tuple-element.596, s32[]{:T(128)} %get-tuple-element.595, f32[35,9,32,32]{0,3,2,1:T(8,128)} %multiply_subtract_fusion.12, f32[35,8,33,32]{0,3,2,1:T(8,128)} %multiply_subtract_fusion.13, f32[35,8,32,33]{0,3,2,1:T(8,128)} %multiply_subtract_fusion.14, ...), kind=kOutput, calls=%fused_computation.12.clone.1 | convolution fusion | flops 122429440 | bytes 33593124 | tf_op jit(solution)/shard_map/while/body/eval_jaxpr/fg,...gzyx->...fzyx/dot_general | solution.py:67
  147.2 4.4 %multiply_subtract_fusion.14 = f32[35,8,32,33]{0,3,2,1:T(8,128)} fusion(f32[35,8,32,1]{0,3,2,1:T(1,128)S(1)} %get-tuple-element.523, f32[35,8,32,32]{0,3,2,1:T(8,128)S(1)} %dynamic-slice_bitcast_fusion.15, f32[35,8,32,1]{0,3,2,1:T(1,128)S(1)} %get-tuple-element.524, f32[35]{0:T(128)S(1)} %get-tuple-element.616, f32[]{:T(128)} %bitcast.137), kind=kLoop, calls=%fused_computation.3.clone.1 | loop fusion | flops 2365440 | bytes 2401424 | tf_op jit(solution)/shard_map/while/body/eval_jaxpr/sub | solution.py:48
  155.6 3.7 multiply_subtract_fusion.12
  159.3 4.6 %constant_dynamic-slice_fusion.4 = f32[1,1,8,32,32]{1,4,3,2,0:T(8,128)} fusion(f32[2,35,8,32,32]{1,4,3,2,0:T(8,128)} %get-tuple-element.613, s32[]{:T(128)} %get-tuple-element.595), kind=kLoop, calls=%fused_computation.26.clone.1 | loop fusion | bytes 65540 | tf_op jit(solution)/shard_map/while/body/eval_jaxpr/slice | solution.py:66
  167.2 14.1 %fusion.78 = f32[2,35,8,32,32]{1,4,3,2,0:T(8,128)} fusion(f32[2,35,8,32,32]{1,4,3,2,0:T(8,128)} %get-tuple-element.596, s32[]{:T(128)} %get-tuple-element.595, f32[35,9,32,32]{0,3,2,1:T(8,128)} %multiply_subtract_fusion.12, f32[35,8,33,32]{0,3,2,1:T(8,128)} %multiply_subtract_fusion.13, f32[35,8,32,33]{0,3,2,1:T(8,128)} %multiply_subtract_fusion.14, ...), kind=kOutput, calls=%fused_computation.12.clone.1 | convolution fusion | flops 122429440 | bytes 33593124 | tf_op jit(solution)/shard_map/while/body/eval_jaxpr/fg,...gzyx->...fzyx/dot_general | solution.py:67
  184.0 12.9 %fusion.42 = (bf16[2,35,8,32,32]{1,4,3,2,0:T(8,128)(2,1)}, f32[2,35,8,32,32]{1,4,3,2,0:T(8,128)}) fusion(f32[2,35,8,32,32]{1,4,3,2,0:T(8,128)} %get-tuple-element.589, f32[2,35,8,32,32]{1,4,3,2,0:T(8,128)} %get-tuple-element.152), kind=kLoop, calls=%fused_computation.120 | loop fusion | flops 1720320 | bytes 8028160 | tf_op jit(solution)/shard_map/convert_element_type | solution.py:155
  199.0 8.6 %collective-permute-start.4 = (bf16[2,35,1,32,32]{1,4,3,2,0:T(8,128)(2,1)}, bf16[2,35,1,32,32]{1,4,3,2,0:T(8,128)(2,1)S(1)}, u32[]{:S(2)}, u32[]{:S(2)}) collective-permute-start(bf16[2,35,1,32,32]{1,4,3,2,0:T(8,128)(2,1)} %get-tuple-element.336), channel_id=1, source_target_pairs={{0,1},{1,2},{2,3},{4,5},{5,6},{6,7},{8,9},{9,10},{10,11},{12,13},{... | collective-permute-start | bytes 430088 | tf_op jit(solution)/shard_map/ppermute | solution.py:17
  215.5 5.8 %pad_maximum_fusion.9 = f32[2,35,10,32,32]{1,4,3,2,0:T(8,128)} fusion(f32[2,35,1,32,32]{1,4,3,2,0:T(8,128)S(1)} %get-tuple-element.333, f32[2,35,8,32,32]{1,4,3,2,0:T(8,128)S(1)} %copy-done, f32[2,35,1,32,32]{1,4,3,2,0:T(8,128)S(1)} %get-tuple-element.332), kind=kLoop, calls=%fused_computation.79 | loop fusion | flops 1433600 | bytes 5734400 | tf_op jit(solution)/shard_map/concatenate | solution.py:158
  221.3 4.4 %broadcast.182 = f32[2,35,8,32,32]{1,4,3,2,0:T(8,128)} broadcast(f32[]{:T(128)} %constant.54.clone.1), dimensions={} | broadcast | bytes 2293764 | tf_op jit(solution)/shard_map/broadcast.31
  225.8 78.0 %while.48 = (s32[]{:T(128)}, f32[2,35,8,32,32]{1,4,3,2,0:T(8,128)}, f32[2,35,8,32]{1,3,2,0:T(8,128)S(1)}, f32[2,35,8,32]{1,3,2,0:T(8,128)S(1)}, f32[2,35,8,32]{1...) while((s32[]{:T(128)}, f32[2,35,8,32,32]{1,4,3,2,0:T(8,128)}, ...), condition=%wide.region_5.6_spmd, body=%wide.region_4.5_spmd.sunk | while | flops 129128448 | bytes 105535960 | solution.py:82
  229.8 4.4 %multiply_subtract_fusion.17 = f32[35,8,32,33]{0,3,2,1:T(8,128)} fusion(f32[35,8,32,1]{0,3,2,1:T(1,128)S(1)} %get-tuple-element.546, f32[35,8,32,32]{0,3,2,1:T(8,128)S(1)} %dynamic-slice_bitcast_fusion.17, f32[35,8,32,1]{0,3,2,1:T(1,128)S(1)} %get-tuple-element.547, f32[35]{0:T(128)S(1)} %get-tuple-element.652, f32[]{:T(128)} %bitcast.150), kind=kLoop, calls=%fused_computation.32.clone.1 | loop fusion | flops 2365440 | bytes 2401424 | tf_op jit(solution)/shard_map/while/body/eval_jaxpr/sub | solution.py:48
  238.3 4.1 %multiply_subtract_fusion.15 = f32[35,9,32,32]{0,3,2,1:T(8,128)} fusion(f32[35,10,32,32]{0,3,2,1:T(8,128)S(1)} %dynamic-slice_bitcast_fusion.16, f32[35]{0:T(128)S(1)} %get-tuple-element.652, f32[]{:T(128)} %bitcast.148), kind=kLoop, calls=%fused_computation.33.clone.1 | loop fusion | flops 1935360 | bytes 3870864 | tf_op jit(solution)/shard_map/while/body/eval_jaxpr/sub | solution.py:48
  248.1 14.1 %fusion.86 = f32[2,35,8,32,32]{1,4,3,2,0:T(8,128)} fusion(f32[2,35,8,32,32]{1,4,3,2,0:T(8,128)} %get-tuple-element.632, s32[]{:T(128)} %get-tuple-element.631, f32[35,9,32,32]{0,3,2,1:T(8,128)} %multiply_subtract_fusion.15, f32[35,8,33,32]{0,3,2,1:T(8,128)} %multiply_subtract_fusion.16, f32[35,8,32,33]{0,3,2,1:T(8,128)} %multiply_subtract_fusion.17, ...), kind=kOutput, calls=%fused_computation.41.clone.1 | convolution fusion | flops 122429440 | bytes 33593124 | tf_op jit(solution)/shard_map/while/body/eval_jaxpr/fg,...gzyx->...fzyx/dot_general | solution.py:67
  268.7 4.4 %multiply_subtract_fusion.17 = f32[35,8,32,33]{0,3,2,1:T(8,128)} fusion(f32[35,8,32,1]{0,3,2,1:T(1,128)S(1)} %get-tuple-element.546, f32[35,8,32,32]{0,3,2,1:T(8,128)S(1)} %dynamic-slice_bitcast_fusion.17, f32[35,8,32,1]{0,3,2,1:T(1,128)S(1)} %get-tuple-element.547, f32[35]{0:T(128)S(1)} %get-tuple-element.652, f32[]{:T(128)} %bitcast.150), kind=kLoop, calls=%fused_computation.32.clone.1 | loop fusion | flops 2365440 | bytes 2401424 | tf_op jit(solution)/shard_map/while/body/eval_jaxpr/sub | solution.py:48
  277.2 4.1 %multiply_subtract_fusion.15 = f32[35,9,32,32]{0,3,2,1:T(8,128)} fusion(f32[35,10,32,32]{0,3,2,1:T(8,128)S(1)} %dynamic-slice_bitcast_fusion.16, f32[35]{0:T(128)S(1)} %get-tuple-element.652, f32[]{:T(128)} %bitcast.148), kind=kLoop, calls=%fused_computation.33.clone.1 | loop fusion | flops 1935360 | bytes 3870864 | tf_op jit(solution)/shard_map/while/body/eval_jaxpr/sub | solution.py:48
  287.0 14.1 %fusion.86 = f32[2,35,8,32,32]{1,4,3,2,0:T(8,128)} fusion(f32[2,35,8,32,32]{1,4,3,2,0:T(8,128)} %get-tuple-element.632, s32[]{:T(128)} %get-tuple-element.631, f32[35,9,32,32]{0,3,2,1:T(8,128)} %multiply_subtract_fusion.15, f32[35,8,33,32]{0,3,2,1:T(8,128)} %multiply_subtract_fusion.16, f32[35,8,32,33]{0,3,2,1:T(8,128)} %multiply_subtract_fusion.17, ...), kind=kOutput, calls=%fused_computation.41.clone.1 | convolution fusion | flops 122429440 | bytes 33593124 | tf_op jit(solution)/shard_map/while/body/eval_jaxpr/fg,...gzyx->...fzyx/dot_general | solution.py:67
  305.6 13.3 %multiply_add_fusion.1 = f32[2,35,8,32,32]{1,4,3,2,0:T(8,128)} fusion(f32[2,35,8,32,32]{1,4,3,2,0:T(8,128)} %get-tuple-element.589, f32[2,35,8,32,32]{1,4,3,2,0:T(8,128)} %get-tuple-element.152, f32[2,35,8,32,32]{1,4,3,2,0:T(8,128)} %get-tuple-element.153), kind=kLoop, calls=%fused_computation.80 | loop fusion | flops 1720320 | bytes 9175040 | tf_op jit(solution)/shard_map/add | solution.py:167
  319.0 7.2 %copy.61 = f32[2,35,8192]{2,0,1:T(2,128)} copy(f32[2,35,8192]{1,2,0:T(8,128)} %bitcast.167) | data formatting | bytes 4587520 | tf_op jit(solution)/shard_map/reshape | solution.py:175
  326.2 57.2 %all-reduce.3.cloned.1.call-done = f32[8,35,256]{2,0,1:T(8,128)} async-done(((f32[8,35,256]{2,0,1:T(8,128)}), f32[8,35,256]{2,0,1:T(8,128)}) %all-reduce.3.cloned.1.call-update) | async-done | bytes 286736
  (179 shorter events, 100.2 us)
Async XLA Ops:
  7.2 376.2 %all-reduce.3.cloned.1.call-start = ((), (), s32[]{:S(2)}) async-start(), calls=%async_computation | async-start | bytes 573440
  7.2 33.6 %copy-start.8 = (s32[2]{0:T(128)}, s32[2]{0:T(128)S(1)}, u32[]{:S(2)}) copy-start(s32[2]{0:T(128)S(1)} %iota_add_fusion.1) | copy-start | bytes 28
  42.5 2.6 collective-permute-start
  43.8 5.0 %collective-permute-start.1 = (bf16[2,35,1,16,16]{1,4,3,2,0:T(8,128)(2,1)S(1)}, bf16[2,35,1,16,16]{1,4,3,2,0:T(8,128)(2,1)S(1)}, u32[]{:S(2)}, u32[]{:S(2)}) collective-permute-start(bf16[2,35,1,16,16]{1,4,3,2,0:T(8,128)(2,1)S(1)} %get-tuple-element.341), channel_id=1, source_target_pairs={{1,0},{2,1},{3,2},{5,4},{6,5},{7,6},{9,8},{10,9},{11,10},{13,12},{... | collective-permute-start | bytes 107528 | tf_op jit(solution)/shard_map/ppermute | solution.py:20
  49.3 4.5 %copy-start.5 = (f32[2]{0:T(128)S(1)}, f32[2]{0:T(128)}, u32[]{:S(2)}) copy-start(f32[2]{0:T(128)} %constant.89.clone..sunk.2) | copy-start | bytes 28
  75.4 2.0 copy-start.1
  77.5 7.0 %collective-permute-start.2 = (bf16[2,35,1,32,32]{1,4,3,2,0:T(8,128)(2,1)S(1)}, bf16[2,35,1,32,32]{1,4,3,2,0:T(8,128)(2,1)S(1)}, u32[]{:S(2)}, u32[]{:S(2)}) collective-permute-start(bf16[2,35,1,32,32]{1,4,3,2,0:T(8,128)(2,1)S(1)} %get-tuple-element.338), channel_id=1, source_target_pairs={{0,1},{1,2},{2,3},{4,5},{5,6},{6,7},{8,9},{9,10},{10,11},{12,13},{... | collective-permute-start | bytes 430088 | tf_op jit(solution)/shard_map/ppermute | solution.py:17
  83.0 3.8 collective-permute-start.3
  97.9 4.5 %copy-start.2 = (f32[35,35]{1,0:T(8,128)S(1)}, f32[35,35]{1,0:T(8,128)}, u32[]{:S(2)}) copy-start(f32[35,35]{1,0:T(8,128)} %param.18) | copy-start | bytes 14704
  97.9 4.5 %copy-start.3 = (f32[35]{0:T(128)S(1)}, f32[35]{0:T(128)}, u32[]{:S(2)}) copy-start(f32[35]{0:T(128)} %param.17) | copy-start | bytes 424
  98.0 4.5 %copy-start.4 = (f32[3]{0:T(128)S(1)}, f32[3]{0:T(128)}, u32[]{:S(2)}) copy-start(f32[3]{0:T(128)} %param.16) | copy-start | bytes 40
  106.5 7.9 %slice-start.5 = ((s8[10485760]{0:T(1024)(128)(4,1)}), s8[4194304]{0:T(1024)(128)(4,1)S(1)}, s32[]{:S(2)}) async-start(s8[10485760]{0:T(1024)(128)(4,1)} %bitcast.163), calls=%async_computation.6 | async-start | bytes 8388608 | tf_op jit(solution)/shard_map/while
  106.5 7.9 %slice-start.6 = ((s8[10485760]{0:T(1024)(128)(4,1)}), s8[4194304]{0:T(1024)(128)(4,1)S(1)}, s32[]{:S(2)}) async-start(s8[10485760]{0:T(1024)(128)(4,1)} %bitcast.163), calls=%async_computation.7 | async-start | bytes 8388608 | tf_op jit(solution)/shard_map/while
  110.9 3.4 slice-start.7
  147.2 7.9 %slice-start.5 = ((s8[10485760]{0:T(1024)(128)(4,1)}), s8[4194304]{0:T(1024)(128)(4,1)S(1)}, s32[]{:S(2)}) async-start(s8[10485760]{0:T(1024)(128)(4,1)} %bitcast.163), calls=%async_computation.6 | async-start | bytes 8388608 | tf_op jit(solution)/shard_map/while
  147.2 7.9 %slice-start.6 = ((s8[10485760]{0:T(1024)(128)(4,1)}), s8[4194304]{0:T(1024)(128)(4,1)S(1)}, s32[]{:S(2)}) async-start(s8[10485760]{0:T(1024)(128)(4,1)} %bitcast.163), calls=%async_computation.7 | async-start | bytes 8388608 | tf_op jit(solution)/shard_map/while
  151.6 3.4 slice-start.7
  184.0 24.9 %copy-start.10 = (u32[32]{0:T(128)S(1)}, u32[32]{0:T(128)}, u32[]{:S(2)}) copy-start(u32[32]{0:T(128)} %constant.94) | copy-start | bytes 388
  199.0 10.6 %collective-permute-start.4 = (bf16[2,35,1,32,32]{1,4,3,2,0:T(8,128)(2,1)}, bf16[2,35,1,32,32]{1,4,3,2,0:T(8,128)(2,1)S(1)}, u32[]{:S(2)}, u32[]{:S(2)}) collective-permute-start(bf16[2,35,1,32,32]{1,4,3,2,0:T(8,128)(2,1)} %get-tuple-element.336), channel_id=1, source_target_pairs={{0,1},{1,2},{2,3},{4,5},{5,6},{6,7},{8,9},{9,10},{10,11},{12,13},{... | collective-permute-start | bytes 430088 | tf_op jit(solution)/shard_map/ppermute | solution.py:17
  207.7 3.8 collective-permute-start.5
  211.5 4.0 %copy-start = (f32[2,35,8,32,32]{1,4,3,2,0:T(8,128)S(1)}, f32[2,35,8,32,32]{1,4,3,2,0:T(8,128)}, u32[]{:S(2)}) copy-start(f32[2,35,8,32,32]{1,4,3,2,0:T(8,128)} %get-tuple-element.625) | copy-start | bytes 6881284
  229.8 7.8 %slice-start.2 = ((s8[10485760]{0:T(1024)(128)(4,1)}), s8[4194304]{0:T(1024)(128)(4,1)S(1)}, s32[]{:S(2)}) async-start(s8[10485760]{0:T(1024)(128)(4,1)} %bitcast.161), calls=%async_computation.3 | async-start | bytes 8388608 | tf_op jit(solution)/shard_map/while
  229.8 7.8 %slice-start.3 = ((s8[10485760]{0:T(1024)(128)(4,1)}), s8[4194304]{0:T(1024)(128)(4,1)S(1)}, s32[]{:S(2)}) async-start(s8[10485760]{0:T(1024)(128)(4,1)} %bitcast.161), calls=%async_computation.4 | async-start | bytes 8388608 | tf_op jit(solution)/shard_map/while
  234.3 3.4 slice-start.4
  237.6 4.7 %slice-start = ((s8[8388608]{0:T(1024)(128)(4,1)}), s8[4194304]{0:T(1024)(128)(4,1)S(1)}, s32[]{:S(2)}) async-start(s8[8388608]{0:T(1024)(128)(4,1)} %bitcast.158), calls=%async_computation.1 | async-start | bytes 8388608 | tf_op jit(solution)/shard_map/while
  238.2 4.1 %slice-start.1 = ((s8[8388608]{0:T(1024)(128)(4,1)}), s8[4194304]{0:T(1024)(128)(4,1)S(1)}, s32[]{:S(2)}) async-start(s8[8388608]{0:T(1024)(128)(4,1)} %bitcast.158), calls=%async_computation.2 | async-start | bytes 8388608 | tf_op jit(solution)/shard_map/while
  268.7 7.8 %slice-start.2 = ((s8[10485760]{0:T(1024)(128)(4,1)}), s8[4194304]{0:T(1024)(128)(4,1)S(1)}, s32[]{:S(2)}) async-start(s8[10485760]{0:T(1024)(128)(4,1)} %bitcast.161), calls=%async_computation.3 | async-start | bytes 8388608 | tf_op jit(solution)/shard_map/while
  268.7 7.8 %slice-start.3 = ((s8[10485760]{0:T(1024)(128)(4,1)}), s8[4194304]{0:T(1024)(128)(4,1)S(1)}, s32[]{:S(2)}) async-start(s8[10485760]{0:T(1024)(128)(4,1)} %bitcast.161), calls=%async_computation.4 | async-start | bytes 8388608 | tf_op jit(solution)/shard_map/while
  273.2 3.4 slice-start.4
  276.5 4.7 %slice-start = ((s8[8388608]{0:T(1024)(128)(4,1)}), s8[4194304]{0:T(1024)(128)(4,1)S(1)}, s32[]{:S(2)}) async-start(s8[8388608]{0:T(1024)(128)(4,1)} %bitcast.158), calls=%async_computation.1 | async-start | bytes 8388608 | tf_op jit(solution)/shard_map/while
  277.1 4.1 %slice-start.1 = ((s8[8388608]{0:T(1024)(128)(4,1)}), s8[4194304]{0:T(1024)(128)(4,1)S(1)}, s32[]{:S(2)}) async-start(s8[8388608]{0:T(1024)(128)(4,1)} %bitcast.158), calls=%async_computation.2 | async-start | bytes 8388608 | tf_op jit(solution)/shard_map/while
  319.0 64.4 %copy-start.6 = (f32[1,35,256]{2,0,1:T(1,128)S(1)}, f32[1,35,256]{2,0,1:T(1,128)}, u32[]{:S(2)}) copy-start(f32[1,35,256]{2,0,1:T(1,128)} %param.14) | copy-start | bytes 107524
  (2 other events, 1.3 us)
Sparse Core Ops, SparseCore 0:
  305.8 77.5 all-reduce.2
where the time goes:
time: 394 us; the launch traced here: 393 us
  other arithmetic  110 us (28%)
  local copies, waits for them, and re-layouts  90.3 us (23%)
  waiting for transfers between devices  65.2 us (17%)
  matrix products  58.5 us (15%)
  blocking collectives  33.6 us (9%)
  starting transfers between devices  19.3 us (5%)
  between operations  14.4 us (4%)
    unnamed x2, waiting for transfers between devices  57.2 us
    dot_general x4, matrix products, tendency(): jnp.einsum('fg,...gzyx->...fzyx', stoich, reaction_rate, precision=highest)  56.3 us
    sub x12, other arithmetic, face_flux(): speed * (left_side + right_side) * 0.5 - diffuse * (right_side - left_side)  46.7 us
    all_gather x1, blocking collectives, shards(): lax.all_gather(coarse_send, 'gx', axis=0, tiled=True)  33.6 us
    convert_element_type x2, other arithmetic, extend_layers(): cells.astype(jnp.bfloat16)  17.4 us
    ppermute x3, starting transfers between devices, padded(): lax.ppermute(lax.slice_in_dim(block, block.shape[dim] - width, None, axis...  15.4 us
    concatenate x2, other arithmetic, extend_layers(): return jnp.concatenate([lower_ghost, cells, upper_ghost], 2)  15.1 us
    squeeze x8, local copies, waits for them, and re-layouts, tendency_slots(): return lax.map(tendency_one_slot, (padded_layers, cells))  14.1 us
  transfers between devices with their start and end apart: 7, of which 5 were waited for; matrix products, arithmetic and copies ran while one was open for 5% of the time, Pallas kernels for 0%

commit v1 on v0

--- a/solution.py
+++ b/solution.py
@@ -131,12 +131,22 @@
     layers = layer_cells // (block_edge * block_edge)
     my_slots = owner_group * own_slots + jnp.arange(own_slots, dtype=jnp.int32)
     chooser = (my_slots[:, None] == patch_owner[None, :]).astype(jnp.bfloat16)
-    gathered = jnp.einsum(
-        "oq,qfc->ofc",
-        chooser,
-        lax.all_gather(coarse_send, "gx", axis=0, tiled=True),
-        preferred_element_type=jnp.float32,
-    )
+    peers, mine, extent = (lax.axis_size("gx"), lax.axis_index("gx"), coarse_send.shape[0])
+    right = [(i_2, (i_2 + 1) % peers) for i_2 in range(peers)]
+    block_2, so_far = (coarse_send, None)
+    for turn in range(peers):
+        upcoming = lax.ppermute(block_2, "gx", right) if turn < peers - 1 else None
+        update = jnp.einsum(
+            "oq,qfc->ofc",
+            lax.dynamic_slice_in_dim(
+                chooser, (mine - turn) % peers * extent, block_2.shape[0], axis=1
+            ),
+            block_2,
+            preferred_element_type=jnp.float32,
+        )
+        so_far = update if so_far is None else so_far + update
+        block_2 = upcoming
+    gathered = so_far
     coarse = gathered.reshape(own_slots, fields, layers, block_edge, block_edge)
     rimmed = padded(coarse.astype(jnp.bfloat16), (("gy", 2),), 1).astype(coarse.dtype)
     below = rimmed[:, :, :-2]

time: 394 us -> 412 us (1.046)
  waiting for transfers between devices: 65.2 us -> 106 us
  blocking collectives: 33.6 us -> 0 us
  local copies, waits for them, and re-layouts: 90.3 us -> 94.9 us
    ppermute x0 -> x7, waiting for transfers between devices: none -> 43.3 us  [shards(): upcoming = lax.ppermute(block_2, 'gx', right) if turn < peers - 1 else None]
    all_gather x1 -> x0, blocking collectives: 33.6 us -> none  [shards(): lax.all_gather(coarse_send, 'gx', axis=0, tiled=True)]
    another operation x11 -> x19, local copies, waits for them, and re-layouts: 13.4 us -> 18.3 us
  transfers between devices with their start and end apart: 7 -> 14, of which waited for: 5 -> 11; matrix products, arithmetic and copies ran while one was open for 5% -> 7% of each run, Pallas kernels for 0% -> 0%
where the time goes in v1:
time: 412 us; the launch traced here: 411 us
  other arithmetic  114 us (28%)
  waiting for transfers between devices  106 us (26%)
  local copies, waits for them, and re-layouts  94.9 us (23%)
  matrix products  57.3 us (14%)
  starting transfers between devices  22.6 us (5%)
  between operations  14.5 us (4%)
    dot_general x4, matrix products, tendency(): jnp.einsum('fg,...gzyx->...fzyx', stoich, reaction_rate, precision=highest)  56.2 us
    unnamed x2, waiting for transfers between devices  53.8 us
    sub x12, other arithmetic, face_flux(): speed * (left_side + right_side) * 0.5 - diffuse * (right_side - left_side)  46.8 us
    ppermute x7, waiting for transfers between devices, shards(): upcoming = lax.ppermute(block_2, 'gx', right) if turn < peers - 1 else None  43.3 us
    another operation x19, local copies, waits for them, and re-layouts  18.3 us
    convert_element_type x2, other arithmetic, extend_layers(): cells.astype(jnp.bfloat16)  17.5 us
    ppermute x3, starting transfers between devices, padded(): lax.ppermute(lax.slice_in_dim(block, block.shape[dim] - width, None, axis...  15.7 us
    concatenate x2, other arithmetic, extend_layers(): return jnp.concatenate([lower_ghost, cells, upper_ghost], 2)  15.1 us
  transfers between devices with their start and end apart: 14, of which 11 were waited for; matrix products, arithmetic and copies ran while one was open for 7% of the time, Pallas kernels for 0%

profile of v1, /device:TPU:0, one launch (start us, length us, event | category | flops | bytes accessed | tf_op | source)
XLA Modules:
  0.0 410.7 jit_solution(10964056232836558018)
XLA Ops:
  16.2 6.9 %collective-permute-done.1 = bf16[1,35,1024]{2,1,0:T(8,128)(2,1)S(1)} collective-permute-done((bf16[1,35,1024]{2,1,0:T(8,128)(2,1)S(1)}, bf16[1,35,1024]{2,1,0:T(8,128)(2,1)S(1)}, u32[]{:S(2)}, u32[]{:S(2)}) %collective-permute-start.1) | collective-permute-done | bytes 71712 | tf_op jit(solution)/shard_map/ppermute | solution.py:138
  23.3 6.9 %collective-permute-done.2 = bf16[1,35,1024]{2,1,0:T(8,128)(2,1)S(1)} collective-permute-done((bf16[1,35,1024]{2,1,0:T(8,128)(2,1)S(1)}, bf16[1,35,1024]{2,1,0:T(8,128)(2,1)S(1)}, u32[]{:S(2)}, u32[]{:S(2)}) %collective-permute-start.2) | collective-permute-done | bytes 71712 | tf_op jit(solution)/shard_map/ppermute | solution.py:138
  30.5 6.9 %collective-permute-done.3 = bf16[1,35,1024]{2,1,0:T(8,128)(2,1)S(1)} collective-permute-done((bf16[1,35,1024]{2,1,0:T(8,128)(2,1)S(1)}, bf16[1,35,1024]{2,1,0:T(8,128)(2,1)S(1)}, u32[]{:S(2)}, u32[]{:S(2)}) %collective-permute-start.3) | collective-permute-done | bytes 71712 | tf_op jit(solution)/shard_map/ppermute | solution.py:138
  38.4 6.1 %collective-permute-done.4 = bf16[1,35,1024]{2,1,0:T(8,128)(2,1)S(1)} collective-permute-done((bf16[1,35,1024]{2,1,0:T(8,128)(2,1)S(1)}, bf16[1,35,1024]{2,1,0:T(8,128)(2,1)S(1)}, u32[]{:S(2)}, u32[]{:S(2)}) %collective-permute-start.4) | collective-permute-done | bytes 71712 | tf_op jit(solution)/shard_map/ppermute | solution.py:138
  45.6 6.6 %collective-permute-done.5 = bf16[1,35,1024]{2,1,0:T(8,128)(2,1)S(1)} collective-permute-done((bf16[1,35,1024]{2,1,0:T(8,128)(2,1)S(1)}, bf16[1,35,1024]{2,1,0:T(8,128)(2,1)S(1)}, u32[]{:S(2)}, u32[]{:S(2)}) %collective-permute-start.5) | collective-permute-done | bytes 71712 | tf_op jit(solution)/shard_map/ppermute | solution.py:138
  53.3 6.1 %collective-permute-done.6 = bf16[1,35,1024]{2,1,0:T(8,128)(2,1)S(1)} collective-permute-done((bf16[1,35,1024]{2,1,0:T(8,128)(2,1)S(1)}, bf16[1,35,1024]{2,1,0:T(8,128)(2,1)S(1)}, u32[]{:S(2)}, u32[]{:S(2)}) %collective-permute-start.6) | collective-permute-done | bytes 71712 | tf_op jit(solution)/shard_map/ppermute | solution.py:138
  69.6 4.5 %broadcast.206.clone = f32[2,35,8,32,32]{1,4,3,2,0:T(8,128)} broadcast(f32[]{:T(128)} %constant.127.clone.1), dimensions={} | broadcast | bytes 2293764 | tf_op jit(solution)/shard_map/broadcast.31
  74.1 17.1 %while.49 = (s32[]{:T(128)}, f32[2,35,8,32,32]{1,4,3,2,0:T(8,128)}, f32[2,35,4,16,16]{1,4,3,2,0:T(8,128)S(1)}, f32[2,35,4,16,16]{1,4,3,2,0:T(8,128)S(1)}, s32[]{:T(128)}, /*index=5*/f32[2]{0:T(128)S(1)}) while((s32[]{:T(128)}, f32[2,35,8,32,32]{1,4,3,2,0:T(8,128)}, f32[2,35,4,16,16]{1,4,3,2,0:T(8,128)S(1)}, ...), condition=%wide.region_1.2_spmd.clone, body=%wide.region_0.1_spmd.sunk.clone.sunk | while | flops 1496322 | bytes 12653153 | solution.py:91
  91.2 4.5 %convert_element_type.22 = bf16[2,35,8,32,32]{1,4,3,2,0:T(8,128)(2,1)S(1)} convert(f32[2,35,8,32,32]{1,4,3,2,0:T(8,128)} %get-tuple-element.593) | non-fusion elementwise | flops 573440 | bytes 3440640 | tf_op jit(solution)/shard_map/convert_element_type | solution.py:165
  99.1 6.1 %collective-permute-start.9 = (bf16[2,35,1,32,32]{1,4,3,2,0:T(8,128)(2,1)S(1)}, bf16[2,35,1,32,32]{1,4,3,2,0:T(8,128)(2,1)S(1)}, u32[]{:S(2)}, u32[]{:S(2)}) collective-permute-start(bf16[2,35,1,32,32]{1,4,3,2,0:T(8,128)(2,1)S(1)} %get-tuple-element.334), channel_id=1, source_target_pairs={{0,1},{1,2},{2,3},{4,5},{5,6},{6,7},{8,9},{9,10},{10,11},{12,13},{... | collective-permute-start | bytes 430088 | tf_op jit(solution)/shard_map/ppermute | solution.py:17
  108.6 9.3 %pad_maximum_fusion.8 = f32[2,35,10,32,32]{1,4,3,2,0:T(8,128)} fusion(f32[2,35,1,32,32]{1,4,3,2,0:T(8,128)S(1)} %get-tuple-element.331, f32[2,35,8,32,32]{1,4,3,2,0:T(8,128)} %get-tuple-element.593, f32[2,35,1,32,32]{1,4,3,2,0:T(8,128)S(1)} %get-tuple-element.330), kind=kLoop, calls=%fused_computation.78 | loop fusion | flops 1433600 | bytes 5734400 | tf_op jit(solution)/shard_map/concatenate | solution.py:168
  117.9 4.4 %broadcast.206.clone.1 = f32[2,35,8,32,32]{1,4,3,2,0:T(8,128)} broadcast(f32[]{:T(128)} %constant.127.clone.1), dimensions={} | broadcast | bytes 2293764 | tf_op jit(solution)/shard_map/broadcast.31
  122.4 81.4 %while.47 = (s32[]{:T(128)}, f32[2,35,8,32,32]{1,4,3,2,0:T(8,128)}, f32[2,35,8,32]{1,3,2,0:T(8,128)S(1)}, f32[2,35,8,32]{1,3,2,0:T(8,128)S(1)}, f32[2,35,8,32]{1...) while((s32[]{:T(128)}, f32[2,35,8,32,32]{1,4,3,2,0:T(8,128)}, ...), condition=%wide.region_3.4_spmd, body=%wide.region_2.3_spmd.sunk | while | flops 129128448 | bytes 80370104 | solution.py:82
  126.4 4.4 %multiply_subtract_fusion.14 = f32[35,8,32,33]{0,3,2,1:T(8,128)} fusion(f32[35,8,32,1]{0,3,2,1:T(1,128)S(1)} %get-tuple-element.527, f32[35,8,32,32]{0,3,2,1:T(8,128)S(1)} %dynamic-slice_bitcast_fusion.15, f32[35,8,32,1]{0,3,2,1:T(1,128)S(1)} %get-tuple-element.528, f32[35]{0:T(128)S(1)} %get-tuple-element.620, f32[]{:T(128)} %bitcast.174), kind=kLoop, calls=%fused_computation.3.clone.1 | loop fusion | flops 2365440 | bytes 2401424 | tf_op jit(solution)/shard_map/while/body/eval_jaxpr/sub | solution.py:48
  138.5 4.6 %constant_dynamic-slice_fusion.12 = f32[1,1,8,32,32]{1,4,3,2,0:T(8,128)} fusion(f32[2,35,8,32,32]{1,4,3,2,0:T(8,128)} %get-tuple-element.617, s32[]{:T(128)} %get-tuple-element.599), kind=kLoop, calls=%fused_computation.26.clone.1 | loop fusion | bytes 65540 | tf_op jit(solution)/shard_map/while/body/eval_jaxpr/slice | solution.py:66
  146.4 14.0 %fusion.88 = f32[2,35,8,32,32]{1,4,3,2,0:T(8,128)} fusion(f32[2,35,8,32,32]{1,4,3,2,0:T(8,128)} %get-tuple-element.600, s32[]{:T(128)} %get-tuple-element.599, f32[35,9,32,32]{0,3,2,1:T(8,128)} %multiply_subtract_fusion.12, f32[35,8,33,32]{0,3,2,1:T(8,128)} %multiply_subtract_fusion.13, f32[35,8,32,33]{0,3,2,1:T(8,128)} %multiply_subtract_fusion.14, ...), kind=kOutput, calls=%fused_computation.12.clone.1 | convolution fusion | flops 122429440 | bytes 33593124 | tf_op jit(solution)/shard_map/while/body/eval_jaxpr/fg,...gzyx->...fzyx/dot_general | solution.py:67
  167.0 4.4 %multiply_subtract_fusion.14 = f32[35,8,32,33]{0,3,2,1:T(8,128)} fusion(f32[35,8,32,1]{0,3,2,1:T(1,128)S(1)} %get-tuple-element.527, f32[35,8,32,32]{0,3,2,1:T(8,128)S(1)} %dynamic-slice_bitcast_fusion.15, f32[35,8,32,1]{0,3,2,1:T(1,128)S(1)} %get-tuple-element.528, f32[35]{0:T(128)S(1)} %get-tuple-element.620, f32[]{:T(128)} %bitcast.174), kind=kLoop, calls=%fused_computation.3.clone.1 | loop fusion | flops 2365440 | bytes 2401424 | tf_op jit(solution)/shard_map/while/body/eval_jaxpr/sub | solution.py:48
  179.2 4.6 %constant_dynamic-slice_fusion.12 = f32[1,1,8,32,32]{1,4,3,2,0:T(8,128)} fusion(f32[2,35,8,32,32]{1,4,3,2,0:T(8,128)} %get-tuple-element.617, s32[]{:T(128)} %get-tuple-element.599), kind=kLoop, calls=%fused_computation.26.clone.1 | loop fusion | bytes 65540 | tf_op jit(solution)/shard_map/while/body/eval_jaxpr/slice | solution.py:66
  187.0 14.1 %fusion.88 = f32[2,35,8,32,32]{1,4,3,2,0:T(8,128)} fusion(f32[2,35,8,32,32]{1,4,3,2,0:T(8,128)} %get-tuple-element.600, s32[]{:T(128)} %get-tuple-element.599, f32[35,9,32,32]{0,3,2,1:T(8,128)} %multiply_subtract_fusion.12, f32[35,8,33,32]{0,3,2,1:T(8,128)} %multiply_subtract_fusion.13, f32[35,8,32,33]{0,3,2,1:T(8,128)} %multiply_subtract_fusion.14, ...), kind=kOutput, calls=%fused_computation.12.clone.1 | convolution fusion | flops 122429440 | bytes 33593124 | tf_op jit(solution)/shard_map/while/body/eval_jaxpr/fg,...gzyx->...fzyx/dot_general | solution.py:67
  203.8 12.9 %fusion.52 = (bf16[2,35,8,32,32]{1,4,3,2,0:T(8,128)(2,1)}, f32[2,35,8,32,32]{1,4,3,2,0:T(8,128)}) fusion(f32[2,35,8,32,32]{1,4,3,2,0:T(8,128)} %get-tuple-element.593, f32[2,35,8,32,32]{1,4,3,2,0:T(8,128)} %get-tuple-element.152), kind=kLoop, calls=%fused_computation.148 | loop fusion | flops 1720320 | bytes 8028160 | tf_op jit(solution)/shard_map/convert_element_type | solution.py:165
  218.9 8.2 %collective-permute-start.11 = (bf16[2,35,1,32,32]{1,4,3,2,0:T(8,128)(2,1)}, bf16[2,35,1,32,32]{1,4,3,2,0:T(8,128)(2,1)S(1)}, u32[]{:S(2)}, u32[]{:S(2)}) collective-permute-start(bf16[2,35,1,32,32]{1,4,3,2,0:T(8,128)(2,1)} %get-tuple-element.332), channel_id=1, source_target_pairs={{0,1},{1,2},{2,3},{4,5},{5,6},{6,7},{8,9},{9,10},{10,11},{12,13},{... | collective-permute-start | bytes 430088 | tf_op jit(solution)/shard_map/ppermute | solution.py:17
  236.9 5.8 %pad_maximum_fusion.9 = f32[2,35,10,32,32]{1,4,3,2,0:T(8,128)} fusion(f32[2,35,1,32,32]{1,4,3,2,0:T(8,128)S(1)} %get-tuple-element.329, f32[2,35,8,32,32]{1,4,3,2,0:T(8,128)S(1)} %copy-done, f32[2,35,1,32,32]{1,4,3,2,0:T(8,128)S(1)} %get-tuple-element.328), kind=kLoop, calls=%fused_computation.79 | loop fusion | flops 1433600 | bytes 5734400 | tf_op jit(solution)/shard_map/concatenate | solution.py:168
  242.7 4.4 %broadcast.206 = f32[2,35,8,32,32]{1,4,3,2,0:T(8,128)} broadcast(f32[]{:T(128)} %constant.127.clone.1), dimensions={} | broadcast | bytes 2293764 | tf_op jit(solution)/shard_map/broadcast.31
  247.2 78.4 %while.48 = (s32[]{:T(128)}, f32[2,35,8,32,32]{1,4,3,2,0:T(8,128)}, f32[2,35,8,32]{1,3,2,0:T(8,128)S(1)}, f32[2,35,8,32]{1,3,2,0:T(8,128)S(1)}, f32[2,35,8,32]{1...) while((s32[]{:T(128)}, f32[2,35,8,32,32]{1,4,3,2,0:T(8,128)}, ...), condition=%wide.region_5.6_spmd, body=%wide.region_4.5_spmd.sunk | while | flops 129128448 | bytes 105535960 | solution.py:82
  251.3 4.4 %multiply_subtract_fusion.17 = f32[35,8,32,33]{0,3,2,1:T(8,128)} fusion(f32[35,8,32,1]{0,3,2,1:T(1,128)S(1)} %get-tuple-element.550, f32[35,8,32,32]{0,3,2,1:T(8,128)S(1)} %dynamic-slice_bitcast_fusion.17, f32[35,8,32,1]{0,3,2,1:T(1,128)S(1)} %get-tuple-element.551, f32[35]{0:T(128)S(1)} %get-tuple-element.656, f32[]{:T(128)} %bitcast.187), kind=kLoop, calls=%fused_computation.32.clone.1 | loop fusion | flops 2365440 | bytes 2401424 | tf_op jit(solution)/shard_map/while/body/eval_jaxpr/sub | solution.py:48
  259.8 4.0 multiply_subtract_fusion.15
  269.7 14.1 %fusion.96 = f32[2,35,8,32,32]{1,4,3,2,0:T(8,128)} fusion(f32[2,35,8,32,32]{1,4,3,2,0:T(8,128)} %get-tuple-element.636, s32[]{:T(128)} %get-tuple-element.635, f32[35,9,32,32]{0,3,2,1:T(8,128)} %multiply_subtract_fusion.15, f32[35,8,33,32]{0,3,2,1:T(8,128)} %multiply_subtract_fusion.16, f32[35,8,32,33]{0,3,2,1:T(8,128)} %multiply_subtract_fusion.17, ...), kind=kOutput, calls=%fused_computation.41.clone.1 | convolution fusion | flops 122429440 | bytes 33593124 | tf_op jit(solution)/shard_map/while/body/eval_jaxpr/fg,...gzyx->...fzyx/dot_general | solution.py:67
  290.4 4.4 %multiply_subtract_fusion.17 = f32[35,8,32,33]{0,3,2,1:T(8,128)} fusion(f32[35,8,32,1]{0,3,2,1:T(1,128)S(1)} %get-tuple-element.550, f32[35,8,32,32]{0,3,2,1:T(8,128)S(1)} %dynamic-slice_bitcast_fusion.17, f32[35,8,32,1]{0,3,2,1:T(1,128)S(1)} %get-tuple-element.551, f32[35]{0:T(128)S(1)} %get-tuple-element.656, f32[]{:T(128)} %bitcast.187), kind=kLoop, calls=%fused_computation.32.clone.1 | loop fusion | flops 2365440 | bytes 2401424 | tf_op jit(solution)/shard_map/while/body/eval_jaxpr/sub | solution.py:48
  308.8 14.1 %fusion.96 = f32[2,35,8,32,32]{1,4,3,2,0:T(8,128)} fusion(f32[2,35,8,32,32]{1,4,3,2,0:T(8,128)} %get-tuple-element.636, s32[]{:T(128)} %get-tuple-element.635, f32[35,9,32,32]{0,3,2,1:T(8,128)} %multiply_subtract_fusion.15, f32[35,8,33,32]{0,3,2,1:T(8,128)} %multiply_subtract_fusion.16, f32[35,8,32,33]{0,3,2,1:T(8,128)} %multiply_subtract_fusion.17, ...), kind=kOutput, calls=%fused_computation.41.clone.1 | convolution fusion | flops 122429440 | bytes 33593124 | tf_op jit(solution)/shard_map/while/body/eval_jaxpr/fg,...gzyx->...fzyx/dot_general | solution.py:67
  327.4 13.4 %multiply_add_fusion.1 = f32[2,35,8,32,32]{1,4,3,2,0:T(8,128)} fusion(f32[2,35,8,32,32]{1,4,3,2,0:T(8,128)} %get-tuple-element.593, f32[2,35,8,32,32]{1,4,3,2,0:T(8,128)} %get-tuple-element.152, f32[2,35,8,32,32]{1,4,3,2,0:T(8,128)} %get-tuple-element.153), kind=kLoop, calls=%fused_computation.80 | loop fusion | flops 1720320 | bytes 9175040 | tf_op jit(solution)/shard_map/add | solution.py:177
  340.7 7.2 %copy.68 = f32[2,35,8192]{2,0,1:T(2,128)} copy(f32[2,35,8192]{1,2,0:T(8,128)} %bitcast.204) | data formatting | bytes 4587520 | tf_op jit(solution)/shard_map/reshape | solution.py:185
  348.0 53.7 %all-reduce.3.cloned.1.call-done = f32[8,35,256]{2,0,1:T(8,128)} async-done(((f32[8,35,256]{2,0,1:T(8,128)}), f32[8,35,256]{2,0,1:T(8,128)}) %all-reduce.3.cloned.1.call-update) | async-done | bytes 286736
  (209 shorter events, 133.9 us)
Async XLA Ops:
  7.2 394.5 %all-reduce.3.cloned.1.call-start = ((), (), s32[]{:S(2)}) async-start(), calls=%async_computation | async-start | bytes 573440
  7.2 8.7 %collective-permute-start = (bf16[1,35,1024]{2,1,0:T(8,128)(2,1)}, bf16[1,35,1024]{2,1,0:T(8,128)(2,1)S(1)}, u32[]{:S(2)}, u32[]{:S(2)}) collective-permute-start(bf16[1,35,1024]{2,1,0:T(8,128)(2,1)} %param.13), channel_id=1, source_target_pairs={{0,4},{4,8},{8,12},{12,16},{16,20},{20,24},{24,28},{28,0},{1,5},{5... | collective-permute-start | bytes 215048 | tf_op jit(solution)/shard_map/ppermute | solution.py:138
  15.9 7.1 %collective-permute-start.1 = (bf16[1,35,1024]{2,1,0:T(8,128)(2,1)S(1)}, bf16[1,35,1024]{2,1,0:T(8,128)(2,1)S(1)}, u32[]{:S(2)}, u32[]{:S(2)}) collective-permute-start(bf16[1,35,1024]{2,1,0:T(8,128)(2,1)S(1)} %collective-permute-done), channel_id=1, source_target_pairs={{0,4},{4,8},{8,12},{12,16},{16,20},{20,24},{24,28},{28,0},{1,5},{5... | collective-permute-start | bytes 215048 | tf_op jit(solution)/shard_map/ppermute | solution.py:138
  23.1 7.1 %collective-permute-start.2 = (bf16[1,35,1024]{2,1,0:T(8,128)(2,1)S(1)}, bf16[1,35,1024]{2,1,0:T(8,128)(2,1)S(1)}, u32[]{:S(2)}, u32[]{:S(2)}) collective-permute-start(bf16[1,35,1024]{2,1,0:T(8,128)(2,1)S(1)} %collective-permute-done.1), channel_id=1, source_target_pairs={{0,4},{4,8},{8,12},{12,16},{16,20},{20,24},{24,28},{28,0},{1,5},{5... | collective-permute-start | bytes 215048 | tf_op jit(solution)/shard_map/ppermute | solution.py:138
  30.2 7.1 %collective-permute-start.3 = (bf16[1,35,1024]{2,1,0:T(8,128)(2,1)S(1)}, bf16[1,35,1024]{2,1,0:T(8,128)(2,1)S(1)}, u32[]{:S(2)}, u32[]{:S(2)}) collective-permute-start(bf16[1,35,1024]{2,1,0:T(8,128)(2,1)S(1)} %collective-permute-done.2), channel_id=1, source_target_pairs={{0,4},{4,8},{8,12},{12,16},{16,20},{20,24},{24,28},{28,0},{1,5},{5... | collective-permute-start | bytes 215048 | tf_op jit(solution)/shard_map/ppermute | solution.py:138
  37.4 7.2 %collective-permute-start.4 = (bf16[1,35,1024]{2,1,0:T(8,128)(2,1)S(1)}, bf16[1,35,1024]{2,1,0:T(8,128)(2,1)S(1)}, u32[]{:S(2)}, u32[]{:S(2)}) collective-permute-start(bf16[1,35,1024]{2,1,0:T(8,128)(2,1)S(1)} %collective-permute-done.3), channel_id=1, source_target_pairs={{0,4},{4,8},{8,12},{12,16},{16,20},{20,24},{24,28},{28,0},{1,5},{5... | collective-permute-start | bytes 215048 | tf_op jit(solution)/shard_map/ppermute | solution.py:138
  44.5 7.7 %collective-permute-start.5 = (bf16[1,35,1024]{2,1,0:T(8,128)(2,1)S(1)}, bf16[1,35,1024]{2,1,0:T(8,128)(2,1)S(1)}, u32[]{:S(2)}, u32[]{:S(2)}) collective-permute-start(bf16[1,35,1024]{2,1,0:T(8,128)(2,1)S(1)} %collective-permute-done.4), channel_id=1, source_target_pairs={{0,4},{4,8},{8,12},{12,16},{16,20},{20,24},{24,28},{28,0},{1,5},{5... | collective-permute-start | bytes 215048 | tf_op jit(solution)/shard_map/ppermute | solution.py:138
  52.2 7.1 %collective-permute-start.6 = (bf16[1,35,1024]{2,1,0:T(8,128)(2,1)S(1)}, bf16[1,35,1024]{2,1,0:T(8,128)(2,1)S(1)}, u32[]{:S(2)}, u32[]{:S(2)}) collective-permute-start(bf16[1,35,1024]{2,1,0:T(8,128)(2,1)S(1)} %collective-permute-done.5), channel_id=1, source_target_pairs={{0,4},{4,8},{8,12},{12,16},{16,20},{20,24},{24,28},{28,0},{1,5},{5... | collective-permute-start | bytes 215048 | tf_op jit(solution)/shard_map/ppermute | solution.py:138
  62.6 2.6 collective-permute-start.7
  63.9 5.1 %collective-permute-start.8 = (bf16[2,35,1,16,16]{1,4,3,2,0:T(8,128)(2,1)S(1)}, bf16[2,35,1,16,16]{1,4,3,2,0:T(8,128)(2,1)S(1)}, u32[]{:S(2)}, u32[]{:S(2)}) collective-permute-start(bf16[2,35,1,16,16]{1,4,3,2,0:T(8,128)(2,1)S(1)} %get-tuple-element.337), channel_id=1, source_target_pairs={{1,0},{2,1},{3,2},{5,4},{6,5},{7,6},{9,8},{10,9},{11,10},{13,12},{... | collective-permute-start | bytes 107528 | tf_op jit(solution)/shard_map/ppermute | solution.py:20
  69.6 4.5 %copy-start.5 = (f32[2]{0:T(128)S(1)}, f32[2]{0:T(128)}, u32[]{:S(2)}) copy-start(f32[2]{0:T(128)} %constant.147.clone..sunk.2) | copy-start | bytes 28
  97.8 7.4 %collective-permute-start.10 = (bf16[2,35,1,32,32]{1,4,3,2,0:T(8,128)(2,1)S(1)}, bf16[2,35,1,32,32]{1,4,3,2,0:T(8,128)(2,1)S(1)}, u32[]{:S(2)}, u32[]{:S(2)}) collective-permute-start(bf16[2,35,1,32,32]{1,4,3,2,0:T(8,128)(2,1)S(1)} %get-tuple-element.335), channel_id=1, source_target_pairs={{1,0},{2,1},{3,2},{5,4},{6,5},{7,6},{9,8},{10,9},{11,10},{13,12},{... | collective-permute-start | bytes 430088 | tf_op jit(solution)/shard_map/ppermute | solution.py:20
  99.1 7.6 %collective-permute-start.9 = (bf16[2,35,1,32,32]{1,4,3,2,0:T(8,128)(2,1)S(1)}, bf16[2,35,1,32,32]{1,4,3,2,0:T(8,128)(2,1)S(1)}, u32[]{:S(2)}, u32[]{:S(2)}) collective-permute-start(bf16[2,35,1,32,32]{1,4,3,2,0:T(8,128)(2,1)S(1)} %get-tuple-element.334), channel_id=1, source_target_pairs={{0,1},{1,2},{2,3},{4,5},{5,6},{6,7},{8,9},{9,10},{10,11},{12,13},{... | collective-permute-start | bytes 430088 | tf_op jit(solution)/shard_map/ppermute | solution.py:17
  117.9 4.5 %copy-start.2 = (f32[35,35]{1,0:T(8,128)S(1)}, f32[35,35]{1,0:T(8,128)}, u32[]{:S(2)}) copy-start(f32[35,35]{1,0:T(8,128)} %param.18) | copy-start | bytes 14704
  117.9 4.5 %copy-start.3 = (f32[35]{0:T(128)S(1)}, f32[35]{0:T(128)}, u32[]{:S(2)}) copy-start(f32[35]{0:T(128)} %param.17) | copy-start | bytes 424
  117.9 4.5 %copy-start.4 = (f32[3]{0:T(128)S(1)}, f32[3]{0:T(128)}, u32[]{:S(2)}) copy-start(f32[3]{0:T(128)} %param.16) | copy-start | bytes 40
  126.4 7.8 %slice-start.5 = ((s8[10485760]{0:T(1024)(128)(4,1)}), s8[4194304]{0:T(1024)(128)(4,1)S(1)}, s32[]{:S(2)}) async-start(s8[10485760]{0:T(1024)(128)(4,1)} %bitcast.200), calls=%async_computation.6 | async-start | bytes 8388608 | tf_op jit(solution)/shard_map/while
  126.4 7.8 %slice-start.6 = ((s8[10485760]{0:T(1024)(128)(4,1)}), s8[4194304]{0:T(1024)(128)(4,1)S(1)}, s32[]{:S(2)}) async-start(s8[10485760]{0:T(1024)(128)(4,1)} %bitcast.200), calls=%async_computation.7 | async-start | bytes 8388608 | tf_op jit(solution)/shard_map/while
  167.0 7.8 %slice-start.5 = ((s8[10485760]{0:T(1024)(128)(4,1)}), s8[4194304]{0:T(1024)(128)(4,1)S(1)}, s32[]{:S(2)}) async-start(s8[10485760]{0:T(1024)(128)(4,1)} %bitcast.200), calls=%async_computation.6 | async-start | bytes 8388608 | tf_op jit(solution)/shard_map/while
  167.0 7.8 %slice-start.6 = ((s8[10485760]{0:T(1024)(128)(4,1)}), s8[4194304]{0:T(1024)(128)(4,1)S(1)}, s32[]{:S(2)}) async-start(s8[10485760]{0:T(1024)(128)(4,1)} %bitcast.200), calls=%async_computation.7 | async-start | bytes 8388608 | tf_op jit(solution)/shard_map/while
  203.8 24.6 %copy-start.10 = (u32[32]{0:T(128)S(1)}, u32[32]{0:T(128)}, u32[]{:S(2)}) copy-start(u32[32]{0:T(128)} %constant.152) | copy-start | bytes 388
  218.9 10.2 %collective-permute-start.11 = (bf16[2,35,1,32,32]{1,4,3,2,0:T(8,128)(2,1)}, bf16[2,35,1,32,32]{1,4,3,2,0:T(8,128)(2,1)S(1)}, u32[]{:S(2)}, u32[]{:S(2)}) collective-permute-start(bf16[2,35,1,32,32]{1,4,3,2,0:T(8,128)(2,1)} %get-tuple-element.332), channel_id=1, source_target_pairs={{0,1},{1,2},{2,3},{4,5},{5,6},{6,7},{8,9},{9,10},{10,11},{12,13},{... | collective-permute-start | bytes 430088 | tf_op jit(solution)/shard_map/ppermute | solution.py:17
  227.1 5.8 %collective-permute-start.12 = (bf16[2,35,1,32,32]{1,4,3,2,0:T(8,128)(2,1)S(1)}, bf16[2,35,1,32,32]{1,4,3,2,0:T(8,128)(2,1)S(1)}, u32[]{:S(2)}, u32[]{:S(2)}) collective-permute-start(bf16[2,35,1,32,32]{1,4,3,2,0:T(8,128)(2,1)S(1)} %get-tuple-element.333), channel_id=1, source_target_pairs={{1,0},{2,1},{3,2},{5,4},{6,5},{7,6},{9,8},{10,9},{11,10},{13,12},{... | collective-permute-start | bytes 430088 | tf_op jit(solution)/shard_map/ppermute | solution.py:20
  251.3 8.0 %slice-start.2 = ((s8[10485760]{0:T(1024)(128)(4,1)}), s8[4194304]{0:T(1024)(128)(4,1)S(1)}, s32[]{:S(2)}) async-start(s8[10485760]{0:T(1024)(128)(4,1)} %bitcast.198), calls=%async_computation.3 | async-start | bytes 8388608 | tf_op jit(solution)/shard_map/while
  251.3 8.0 %slice-start.3 = ((s8[10485760]{0:T(1024)(128)(4,1)}), s8[4194304]{0:T(1024)(128)(4,1)S(1)}, s32[]{:S(2)}) async-start(s8[10485760]{0:T(1024)(128)(4,1)} %bitcast.198), calls=%async_computation.4 | async-start | bytes 8388608 | tf_op jit(solution)/shard_map/while
  259.2 4.7 %slice-start = ((s8[8388608]{0:T(1024)(128)(4,1)}), s8[4194304]{0:T(1024)(128)(4,1)S(1)}, s32[]{:S(2)}) async-start(s8[8388608]{0:T(1024)(128)(4,1)} %bitcast.195), calls=%async_computation.1 | async-start | bytes 8388608 | tf_op jit(solution)/shard_map/while
  259.8 4.1 slice-start.1
  290.4 8.0 %slice-start.2 = ((s8[10485760]{0:T(1024)(128)(4,1)}), s8[4194304]{0:T(1024)(128)(4,1)S(1)}, s32[]{:S(2)}) async-start(s8[10485760]{0:T(1024)(128)(4,1)} %bitcast.198), calls=%async_computation.3 | async-start | bytes 8388608 | tf_op jit(solution)/shard_map/while
  290.4 8.0 %slice-start.3 = ((s8[10485760]{0:T(1024)(128)(4,1)}), s8[4194304]{0:T(1024)(128)(4,1)S(1)}, s32[]{:S(2)}) async-start(s8[10485760]{0:T(1024)(128)(4,1)} %bitcast.198), calls=%async_computation.4 | async-start | bytes 8388608 | tf_op jit(solution)/shard_map/while
  298.3 4.7 %slice-start = ((s8[8388608]{0:T(1024)(128)(4,1)}), s8[4194304]{0:T(1024)(128)(4,1)S(1)}, s32[]{:S(2)}) async-start(s8[8388608]{0:T(1024)(128)(4,1)} %bitcast.195), calls=%async_computation.1 | async-start | bytes 8388608 | tf_op jit(solution)/shard_map/while
  298.9 4.1 slice-start.1
  340.7 61.0 %copy-start.6 = (f32[1,35,256]{2,0,1:T(1,128)S(1)}, f32[1,35,256]{2,0,1:T(1,128)}, u32[]{:S(2)}) copy-start(f32[1,35,256]{2,0,1:T(1,128)} %param.14) | copy-start | bytes 107524
  (9 other events, 22.0 us)
Sparse Core Ops, SparseCore 0:
  327.5 74.1 all-reduce.2
